TPU v7x, 32 devices: a whole 2x2x4 slice. The times are simulated.
32 devices in a mesh: parts: 2 (over y), col: 16 (over z, x, core).
Axes of the slice: x: 2, y: 2, z: 4, core: 2. Of those that a mesh axis runs over, the one named last changes fastest.
Arguments:
- alignment_rows: bfloat16 [128, 128, 256], P('parts', 'col'), parts along dimension 0, may hold values from -6 to 6
- alignment_columns: bfloat16 [128, 256, 256], P('parts', 'col'), parts along dimension 0, may hold values from -6 to 6
- slab_alignment_mask: int32 [128, 128], P('parts'), parts along dimension 0, may hold values 0 or 1
- slab_crop_mask: int32 [256], P('parts'), parts along dimension 0, may hold values 0 or 1
- column_alignment_mask: int32 [128, 256], P('parts', 'col'), parts along dimension 0, may hold values 0 or 1
- column_crop_mask: int32 [512], P(('parts', 'col')), parts along dimension 0, may hold values 0 or 1
- norm_scale_gain: float32 [256], replicated, may hold values from 0.25 to 1.75
- norm_offset_bias: float32 [256], replicated, may hold values from -3 to 3
- left_projection_weight: bfloat16 [256, 32], replicated, may hold values from -0.375 to 0.375
- right_projection_weight: bfloat16 [256, 32], replicated, may hold values from -0.375 to 0.375
- pair_output_weight: bfloat16 [1024, 128], replicated, may hold values from -1.5 to 1.5
- pair_output_bias: float32 [128], replicated, may hold values from -3 to 3
- pair_update_gradient: bfloat16 [256, 256, 128], P('parts', 'col'), parts along dimension 0, may hold values from -4 to 4
Outputs:
- pair_out: bfloat16 [256, 256, 128], P('parts', 'col'), parts along dimension 0
- grad_rows: bfloat16 [128, 128, 256], P('parts', 'col'), parts along dimension 0
- grad_cols: bfloat16 [128, 256, 256], P('parts', 'col'), parts along dimension 0
- grad_pair_weight: float32 [2048, 128], P(('parts', 'col')), parts along dimension 0
- grad_proj: float32 [512, 64], P(('parts', 'col')), parts along dimension 0
There are 2 independent parts, one for each index of `parts`. A program takes and returns all parts, laid end to end along the dimension named above; an argument that names none is the same for every part. Nothing has to cross between parts.
All inputs are finite; a program needn't handle non-finite values. No bound on the sum of `column_alignment_mask` or of `column_crop_mask` on one device may be relied on, other than what follows from the above.
Results may differ from a plain program's by a relative error of at most 0.007.
Values may be sent and summed in bfloat16 or wider, within the bound.
A program may use at most 128 MiB of HBM per device.

v0:
```python
import jax
import jax.numpy as jnp
from jax import lax
from jax.sharding import PartitionSpec as P

ALIGNMENT_WIDTH = 256
PROJECTED_WIDTH = 32
PAIR_WIDTH = 128
ALIGNMENT_COUNT = 64
SLAB_ROW_COUNT = 128
COLUMN_RESIDUES = 16
norm_eps = 1e-05
row_block_inputs = 64


def apply_layer_norm(value_array, gain, shift):
    value_array = value_array.astype(jnp.float32)
    center = value_array - jnp.mean(value_array, axis=-1, keepdims=True)
    spread = jnp.mean(center * center, axis=-1, keepdims=True)
    return center * lax.rsqrt(spread + norm_eps) * gain + shift


def per_device(
    alignment_rows,
    alignment_columns,
    slab_alignment_mask,
    slab_crop_mask,
    column_alignment_mask,
    column_crop_mask,
    norm_scale_gain,
    norm_offset_bias,
    left_projection_weight,
    right_projection_weight,
    pair_output_weight,
    pair_output_bias,
    pair_update_gradient,
):
    local_rows = alignment_rows.shape[1]
    position = lax.axis_index("col")
    row_mask_weight = (slab_alignment_mask * slab_crop_mask[None, :]).astype(jnp.float32)
    local_mask_weight = lax.dynamic_slice_in_dim(
        row_mask_weight, position * local_rows, local_rows, 1
    )
    column_mask_weight = (column_alignment_mask * column_crop_mask[None, :]).astype(jnp.float32)
    normalized_rows = apply_layer_norm(alignment_rows, norm_scale_gain, norm_offset_bias).astype(
        jnp.bfloat16
    )
    normalized_columns = apply_layer_norm(
        alignment_columns, norm_scale_gain, norm_offset_bias
    ).astype(jnp.bfloat16)
    left_local_factor = jnp.dot(
        normalized_rows.reshape(-1, ALIGNMENT_WIDTH),
        left_projection_weight,
        preferred_element_type=jnp.float32,
    )
    left_local_factor = (
        left_local_factor.reshape(ALIGNMENT_COUNT, local_rows, PROJECTED_WIDTH)
        * local_mask_weight[:, :, None]
    ).astype(jnp.bfloat16)
    left_outgoing = left_local_factor.transpose(1, 0, 2).reshape(
        local_rows, ALIGNMENT_COUNT * PROJECTED_WIDTH
    )
    right_factor = jnp.dot(
        normalized_columns.reshape(-1, ALIGNMENT_WIDTH),
        right_projection_weight,
        preferred_element_type=jnp.float32,
    )
    right_factor = (
        right_factor.reshape(ALIGNMENT_COUNT, COLUMN_RESIDUES, PROJECTED_WIDTH)
        * column_mask_weight[:, :, None]
    ).astype(jnp.bfloat16)
    denom = jnp.maximum(
        jnp.dot(
            row_mask_weight.T,
            column_mask_weight,
            precision=lax.Precision.HIGHEST,
            preferred_element_type=jnp.float32,
        ),
        1.0,
    )
    weight_back = pair_output_weight.T

    def outer_rows(remaining_rows, rows_denom):
        outer = (
            jnp.einsum(
                "isc,sjd->ijcd", remaining_rows, right_factor, preferred_element_type=jnp.float32
            )
            / rows_denom[:, :, None, None]
        )
        return outer.astype(jnp.bfloat16).reshape(-1, PROJECTED_WIDTH * PROJECTED_WIDTH)

    def outer_grad(rows_grad, rows_denom, row_inputs):
        grad_flat = rows_grad.reshape(-1, PAIR_WIDTH)
        grad_outer = (
            jnp.dot(grad_flat, weight_back, preferred_element_type=jnp.float32)
            / rows_denom.reshape(-1, 1)
        ).astype(jnp.bfloat16)
        return (
            grad_flat,
            grad_outer.reshape(row_inputs, COLUMN_RESIDUES, PROJECTED_WIDTH, PROJECTED_WIDTH),
        )

    def make_step():

        def step(carry, item):
            weight_sum, right_sum = carry
            remaining_rows, rows_denom, rows_grad = item
            flat = outer_rows(remaining_rows, rows_denom)
            grad_flat, grad_four = outer_grad(rows_grad, rows_denom, row_block_inputs)
            weight_sum = weight_sum + jnp.einsum(
                "nc,np->cp", flat, grad_flat, preferred_element_type=jnp.float32
            )
            right_sum = right_sum + jnp.einsum(
                "ijcd,isc->sjd", grad_four, remaining_rows, preferred_element_type=jnp.float32
            )
            extra = ()
            extra = extra + (
                jnp.einsum(
                    "ijcd,sjd->isc", grad_four, right_factor, preferred_element_type=jnp.float32
                ),
            )
            return ((weight_sum, right_sum), extra)

        return step

    mask_count_total = SLAB_ROW_COUNT // row_block_inputs
    denom_blocks = denom.reshape(mask_count_total, row_block_inputs, COLUMN_RESIDUES)
    grad_blocks = pair_update_gradient.reshape(
        mask_count_total, row_block_inputs, COLUMN_RESIDUES, PAIR_WIDTH
    )
    start_index = (
        jnp.zeros((PROJECTED_WIDTH * PROJECTED_WIDTH, PAIR_WIDTH), jnp.float32),
        jnp.zeros((ALIGNMENT_COUNT, COLUMN_RESIDUES, PROJECTED_WIDTH), jnp.float32),
    )
    current_piece = lax.all_gather(left_outgoing, "col", axis=0, tiled=True)
    row_inputs = current_piece.shape[0]
    remaining_rows = current_piece.reshape(row_inputs, ALIGNMENT_COUNT, PROJECTED_WIDTH)
    rows_denom = denom
    pair = (
        jnp.dot(
            outer_rows(remaining_rows, rows_denom),
            pair_output_weight,
            preferred_element_type=jnp.float32,
        )
        + pair_output_bias
    )
    pair_out = pair.astype(jnp.bfloat16).reshape(row_inputs, COLUMN_RESIDUES, PAIR_WIDTH)
    collected_blocks = lax.all_gather(left_outgoing, "col", axis=0, tiled=True)
    left_factor_blocks = collected_blocks.reshape(
        mask_count_total, row_block_inputs, ALIGNMENT_COUNT, PROJECTED_WIDTH
    )
    (weight_sum, right_sum), step_outputs = lax.scan(
        make_step(), start_index, (left_factor_blocks, denom_blocks, grad_blocks)
    )
    left_product_terms = step_outputs[0].reshape(SLAB_ROW_COUNT, ALIGNMENT_COUNT * PROJECTED_WIDTH)
    left_total_sum = lax.psum_scatter(left_product_terms, "col", scatter_dimension=0, tiled=True)
    left_total_sum = left_total_sum.reshape(local_rows, ALIGNMENT_COUNT, PROJECTED_WIDTH).transpose(
        1, 0, 2
    )
    left_side_gradient = (left_total_sum * local_mask_weight[:, :, None]).astype(jnp.bfloat16)
    right_side_gradient = (right_sum * column_mask_weight[:, :, None]).astype(jnp.bfloat16)
    projected_left = jnp.einsum(
        "nm,nc->mc",
        normalized_rows.reshape(-1, ALIGNMENT_WIDTH),
        left_side_gradient.reshape(-1, PROJECTED_WIDTH),
        preferred_element_type=jnp.float32,
    )
    projected_right = jnp.einsum(
        "nm,nc->mc",
        normalized_columns.reshape(-1, ALIGNMENT_WIDTH),
        right_side_gradient.reshape(-1, PROJECTED_WIDTH),
        preferred_element_type=jnp.float32,
    )
    proj_terms = jnp.concatenate([projected_left, projected_right], axis=1)
    grad_pair_weight, grad_proj = (
        lax.psum_scatter(weight_sum, "col", scatter_dimension=0, tiled=True),
        lax.psum_scatter(proj_terms, "col", scatter_dimension=0, tiled=True),
    )
    normalized_row_gradient = jnp.dot(
        left_side_gradient.reshape(-1, PROJECTED_WIDTH),
        left_projection_weight.T,
        preferred_element_type=jnp.float32,
    ).reshape(ALIGNMENT_COUNT, local_rows, ALIGNMENT_WIDTH)
    normalized_column_gradient = jnp.dot(
        right_side_gradient.reshape(-1, PROJECTED_WIDTH),
        right_projection_weight.T,
        preferred_element_type=jnp.float32,
    ).reshape(ALIGNMENT_COUNT, COLUMN_RESIDUES, ALIGNMENT_WIDTH)
    unused_result, row_back_grads = jax.vjp(
        lambda value_array: apply_layer_norm(value_array, norm_scale_gain, norm_offset_bias),
        alignment_rows.astype(jnp.float32),
    )
    unused_result, column_back_grads = jax.vjp(
        lambda value_array: apply_layer_norm(value_array, norm_scale_gain, norm_offset_bias),
        alignment_columns.astype(jnp.float32),
    )
    grad_rows = row_back_grads(normalized_row_gradient)[0].astype(jnp.bfloat16)
    grad_cols = column_back_grads(normalized_column_gradient)[0].astype(jnp.bfloat16)
    return (pair_out, grad_rows, grad_cols, grad_pair_weight, grad_proj)


def solution(mesh):
    placed = (
        P("parts", "col", None),
        P("parts", "col", None),
        P("parts", None),
        P("parts"),
        P("parts", "col"),
        P(("parts", "col")),
        P(),
        P(),
        P(),
        P(),
        P(),
        P(),
        P("parts", "col", None),
    )
    return jax.shard_map(
        per_device,
        mesh=mesh,
        in_specs=placed,
        out_specs=(
            P("parts", "col", None),
            P("parts", "col", None),
            P("parts", "col", None),
            P(("parts", "col"), None),
            P(("parts", "col"), None),
        ),
        check_vma=False,
    )
```

profile of v0, /device:TPU:0, one launch (start us, length us, event | category | flops | bytes accessed | tf_op | source)
XLA Modules:
  0.0 399.0 jit_solution(2750851517956724560)
XLA Ops:
  7.3 0.9 multiply_convert_fusion.4
  8.3 0.8 multiply_convert_fusion.3
  9.9 1.1 convert_reduce_fusion.1
  11.0 1.2 fusion.35
  12.2 1.3 convert_reduce_fusion
  13.5 1.4 fusion.26
  15.5 1.3 fusion.25
  17.6 0.9 copy.110
  18.5 0.8 copy.108
  19.4 24.6 %all_gather.4 = bf16[128,2048]{1,0:T(8,128)(2,1)S(1)} all-gather(bf16[8,2048]{1,0:T(8,128)(2,1)S(1)} %reshape.128), channel_id=1, replica_groups=mesh['parts'=2,'col'=16] {'col'}, dimensions={0}, use_global_device_ids=true | all-gather | bytes 557056 | tf_op jit(solution)/shard_map/all_gather | solution.py:135
  44.7 2.3 copy.109
  47.0 168.8 %while.15 = (s32[]{:T(128)}, f32[1024,128]{1,0:T(8,128)S(1)}, f32[64,16,32]{0,2,1:T(8,128)}, f32[2,64,64,32]{1,0,3,2:T(2,128)}, bf16[2,64,64,32]{2,1,3,0:T(8,128...) while((s32[]{:T(128)}, f32[1024,128]{1,0:T(8,128)S(1)}, ...), condition=%wide.region_5.6_spmd.clone, body=%wide.region_4.5_spmd.clone.sunk | while | flops 944046080 | bytes 43880792 | solution.py:152
  47.4 3.1 divide_convert_fusion.3
  50.5 3.3 fusion.90
  53.7 13.4 %copy.160 = bf16[64,16,32,32]{3,2,1,0:T(8,128)(2,1)} copy(bf16[64,16,32,32]{0,3,1,2:T(8,128)(2,1)} %fusion.90) | data formatting | bytes 4194304 | tf_op jit(solution)/shard_map/while/body/eval_jaxpr/convert_element_type | solution.py:90
  67.1 11.3 %reshape.156 = bf16[1024,1024]{1,0:T(8,128)(2,1)S(1)} reshape(bf16[64,16,32,32]{3,2,1,0:T(8,128)(2,1)} %copy.160) | data formatting | bytes 4194304 | tf_op jit(solution)/shard_map/while/body/eval_jaxpr/reshape | solution.py:90
  78.4 0.8 convolution_add_fusion.3
  79.3 11.1 %reshape.157 = bf16[64,16,32,32]{3,2,1,0:T(8,128)(2,1)} reshape(bf16[1024,1024]{1,0:T(8,128)(2,1)} %divide_convert_fusion.3) | data formatting | bytes 4194304 | tf_op jit(solution)/shard_map/while/body/eval_jaxpr/reshape | solution.py:100
  90.4 13.0 %fusion.91 = f32[64,16,32]{0,2,1:T(8,128)S(1)} fusion(bf16[64,16,32,32]{3,2,1,0:T(8,128)(2,1)} %reshape.157, bf16[2,64,64,32]{2,1,3,0:T(8,128)(2,1)S(1)} %copy-done.10, s32[]{:T(128)S(6)} %copy.168, f32[64,16,32]{0,2,1:T(8,128)S(1)} %copy-done.25, pred[]{:T(512)S(6)} %compare.3), kind=kOutput, calls=%fused_computation.8.clone.1 | convolution fusion | flops 134283264 | bytes 3014661 | tf_op jit(solution)/shard_map/while/body/eval_jaxpr/ijcd,isc->sjd/dot_general | solution.py:113
  103.5 1.7 convolution_bitcast_fusion.5
  105.2 0.8 copy.162
  106.0 25.5 %dynamic_update_slice.6 = f32[2,64,64,32]{1,0,3,2:T(2,128)} dynamic-update-slice(f32[2,64,64,32]{1,0,3,2:T(2,128)} %get-tuple-element.248, f32[1,64,64,32]{1,0,3,2:T(1,128)S(1)} %copy.162, s32[]{:T(128)S(6)} %copy.168, s32[]{:T(128)} %constant.21.clone.1..sunk, s32[]{:T(128)} %constant.21.clone.1..sunk, s32[]{:T(128)} %constant.21.clone.1..sunk) | dynamic-update-slice | bytes 1048580 | tf_op jit(solution)/shard_map/while/body/jit(dynamic_update_index_in_dim)/dynamic_update_slice | solution.py:152
  131.7 3.1 divide_convert_fusion.3
  134.8 3.3 fusion.90
  138.0 13.4 %copy.160 = bf16[64,16,32,32]{3,2,1,0:T(8,128)(2,1)} copy(bf16[64,16,32,32]{0,3,1,2:T(8,128)(2,1)} %fusion.90) | data formatting | bytes 4194304 | tf_op jit(solution)/shard_map/while/body/eval_jaxpr/convert_element_type | solution.py:90
  151.4 11.3 %reshape.156 = bf16[1024,1024]{1,0:T(8,128)(2,1)S(1)} reshape(bf16[64,16,32,32]{3,2,1,0:T(8,128)(2,1)} %copy.160) | data formatting | bytes 4194304 | tf_op jit(solution)/shard_map/while/body/eval_jaxpr/reshape | solution.py:90
  162.7 0.8 convolution_add_fusion.3
  163.6 11.1 %reshape.157 = bf16[64,16,32,32]{3,2,1,0:T(8,128)(2,1)} reshape(bf16[1024,1024]{1,0:T(8,128)(2,1)} %divide_convert_fusion.3) | data formatting | bytes 4194304 | tf_op jit(solution)/shard_map/while/body/eval_jaxpr/reshape | solution.py:100
  174.7 13.0 %fusion.91 = f32[64,16,32]{0,2,1:T(8,128)S(1)} fusion(bf16[64,16,32,32]{3,2,1,0:T(8,128)(2,1)} %reshape.157, bf16[2,64,64,32]{2,1,3,0:T(8,128)(2,1)S(1)} %copy-done.10, s32[]{:T(128)S(6)} %copy.168, f32[64,16,32]{0,2,1:T(8,128)S(1)} %copy-done.25, pred[]{:T(512)S(6)} %compare.3), kind=kOutput, calls=%fused_computation.8.clone.1 | convolution fusion | flops 134283264 | bytes 3014661 | tf_op jit(solution)/shard_map/while/body/eval_jaxpr/ijcd,isc->sjd/dot_general | solution.py:113
  187.8 1.7 convolution_bitcast_fusion.5
  189.5 0.8 copy.162
  190.3 25.5 %dynamic_update_slice.6 = f32[2,64,64,32]{1,0,3,2:T(2,128)} dynamic-update-slice(f32[2,64,64,32]{1,0,3,2:T(2,128)} %get-tuple-element.248, f32[1,64,64,32]{1,0,3,2:T(1,128)S(1)} %copy.162, s32[]{:T(128)S(6)} %copy.168, s32[]{:T(128)} %constant.21.clone.1..sunk, s32[]{:T(128)} %constant.21.clone.1..sunk, s32[]{:T(128)} %constant.21.clone.1..sunk) | dynamic-update-slice | bytes 1048580 | tf_op jit(solution)/shard_map/while/body/jit(dynamic_update_index_in_dim)/dynamic_update_slice | solution.py:152
  215.8 2.8 reshape.135
  218.7 1.3 copy.128
  220.1 0.7 reduce-scatter.8.cloned.1.call-update
  221.3 0.8 convolution_bitcast_fusion.2
  222.7 0.6 fusion.42
  223.4 1.4 add_convert_fusion
  224.8 3.2 fusion.17
  228.0 23.0 %copy.106 = bf16[128,16,32,32]{3,2,1,0:T(8,128)(2,1)} copy(bf16[128,16,32,32]{0,3,2,1:T(8,128)(2,1)} %fusion.17) | data formatting | bytes 8388608 | tf_op jit(solution)/shard_map/convert_element_type | solution.py:90
  251.1 23.3 %reshape.130 = bf16[2048,1024]{1,0:T(8,128)(2,1)} reshape(bf16[128,16,32,32]{3,2,1,0:T(8,128)(2,1)} %copy.106) | data formatting | bytes 8388608 | tf_op jit(solution)/shard_map/reshape | solution.py:90
  274.4 4.3 %fusion.18 = bf16[2048,128]{1,0:T(8,128)(2,1)} fusion(bf16[2048,1024]{1,0:T(8,128)(2,1)} %reshape.130, bf16[1024,128]{1,0:T(8,128)(2,1)S(1)} %copy-done.31, f32[128]{0:T(128)S(1)} %copy-done.43), kind=kOutput, calls=%fused_computation.22 | convolution fusion | flops 537395200 | bytes 4981248 | tf_op jit(solution)/shard_map/dot_general | solution.py:140
  278.7 1.2 copy.129
  279.9 0.6 copy.114
  281.1 0.8 copy.130
  282.6 1.0 add_convert_fusion.1
  283.6 50.7 %reduce-scatter.8.cloned.1.call-done = f32[64,128]{1,0:T(8,128)} async-done(((f32[1024,128]{1,0:T(8,128)}), f32[64,128]{1,0:T(8,128)}) %reduce-scatter.8.cloned.1.call-update) | async-done | bytes 32784 | tf_op jit(solution)/shard_map/reduce_scatter | solution.py:176
  334.3 58.2 %reduce-scatter.12.cloned.1.call-done = f32[16,64]{1,0:T(8,128)} async-done(((f32[256,64]{1,0:T(8,128)}), f32[16,64]{1,0:T(8,128)}) %reduce-scatter.12.cloned.1.call-update) | async-done | bytes 4112
  (146 shorter events, 5.8 us)
Async XLA Ops:
  7.2 9.9 %copy-start = (bf16[256,32]{0,1:T(8,128)(2,1)S(1)}, bf16[256,32]{0,1:T(8,128)(2,1)}, u32[]{:S(2)}) copy-start(bf16[256,32]{0,1:T(8,128)(2,1)} %param.24) | copy-start | bytes 49156
  7.2 9.9 %copy-start.3 = (bf16[64,16,256]{2,1,0:T(8,128)(2,1)S(1)}, bf16[64,16,256]{2,1,0:T(8,128)(2,1)}, u32[]{:S(2)}) copy-start(bf16[64,16,256]{2,1,0:T(8,128)(2,1)} %param.16) | copy-start | bytes 1572868
  7.2 9.9 %copy-start.39 = (f32[256]{0:T(256)S(1)}, f32[256]{0:T(256)}, u32[]{:S(2)}) copy-start(f32[256]{0:T(256)} %param.21) | copy-start | bytes 3076
  7.2 9.9 %copy-start.41 = (f32[256]{0:T(256)S(1)}, f32[256]{0:T(256)}, u32[]{:S(2)}) copy-start(f32[256]{0:T(256)} %param.22) | copy-start | bytes 3076
  7.2 11.3 %copy-start.30 = (bf16[1024,128]{1,0:T(8,128)(2,1)S(1)}, bf16[1024,128]{1,0:T(8,128)(2,1)}, u32[]{:S(2)}) copy-start(bf16[1024,128]{1,0:T(8,128)(2,1)} %param.25) | copy-start | bytes 786436
  7.2 271.5 %reduce-scatter.10.cloned.1.call-start = ((), (), s32[]{:S(2)}) async-start(), calls=%async_computation.4 | async-start | bytes 1114112
  8.3 36.0 %copy-start.32 = (f32[64,16]{1,0:T(8,128)}, f32[64,16]{1,0:T(8,128)S(1)}, u32[]{:S(2)}) copy-start(f32[64,16]{1,0:T(8,128)S(1)} %copy.101) | copy-start | bytes 12292
  11.0 32.9 %copy-start.13 = (f32[64,8]{1,0:T(8,128)}, f32[64,8]{1,0:T(8,128)S(1)}, u32[]{:S(2)}) copy-start(f32[64,8]{1,0:T(8,128)S(1)} %broadcast_multiply_fusion) | copy-start | bytes 6148
  12.2 31.7 %copy-start.19 = (f32[64,8]{1,0:T(8,128)}, f32[64,8]{1,0:T(8,128)S(1)}, u32[]{:S(2)}) copy-start(f32[64,8]{1,0:T(8,128)S(1)} %fusion.35) | copy-start | bytes 6148
  12.2 31.7 %copy-start.17 = (f32[64,8]{1,0:T(8,128)}, f32[64,8]{1,0:T(8,128)S(1)}, u32[]{:S(2)}) copy-start(f32[64,8]{1,0:T(8,128)S(1)} %fusion.51) | copy-start | bytes 6148
  13.5 31.1 %copy-start.11 = (f32[64,16]{1,0:T(8,128)}, f32[64,16]{1,0:T(8,128)S(1)}, u32[]{:S(2)}) copy-start(f32[64,16]{1,0:T(8,128)S(1)} %broadcast_multiply_fusion.1) | copy-start | bytes 12292
  15.5 31.4 %copy-start.21 = (f32[64,16]{1,0:T(8,128)}, f32[64,16]{1,0:T(8,128)S(1)}, u32[]{:S(2)}) copy-start(f32[64,16]{1,0:T(8,128)S(1)} %fusion.50) | copy-start | bytes 12292
  16.9 30.1 %copy-start.6 = (bf16[128,16,128]{2,1,0:T(8,128)(2,1)S(1)}, bf16[128,16,128]{2,1,0:T(8,128)(2,1)}, u32[]{:S(2)}) copy-start(bf16[128,16,128]{2,1,0:T(8,128)(2,1)} %param.27) | copy-start | bytes 1572868
  17.6 26.3 %copy-start.28 = (bf16[64,16,32]{2,1,0:T(8,128)(2,1)}, bf16[64,16,32]{2,1,0:T(8,128)(2,1)S(1)}, u32[]{:S(2)}) copy-start(bf16[64,16,32]{2,1,0:T(8,128)(2,1)S(1)} %fusion.23) | copy-start | bytes 196612
  47.4 3.1 copy-start.9
  47.4 3.1 copy-start.34
  79.3 11.1 %copy-start.10 = (bf16[2,64,64,32]{2,1,3,0:T(8,128)(2,1)S(1)}, bf16[2,64,64,32]{2,1,3,0:T(8,128)(2,1)}, u32[]{:S(2)}) copy-start(bf16[2,64,64,32]{2,1,3,0:T(8,128)(2,1)} %get-tuple-element.260) | copy-start | bytes 1572868 | tf_op jit(solution)/shard_map/while
  79.3 11.1 %copy-start.25 = (f32[64,16,32]{0,2,1:T(8,128)S(1)}, f32[64,16,32]{0,2,1:T(8,128)}, u32[]{:S(2)}) copy-start(f32[64,16,32]{0,2,1:T(8,128)} %get-tuple-element.247) | copy-start | bytes 393220 | tf_op jit(solution)/shard_map/while
  90.4 13.1 %copy-start.1 = (bf16[64,16,32,32]{3,2,1,0:T(8,128)(2,1)S(1)}, bf16[64,16,32,32]{3,2,1,0:T(8,128)(2,1)}, u32[]{:S(2)}) copy-start(bf16[64,16,32,32]{3,2,1,0:T(8,128)(2,1)} %reshape.157) | copy-start | bytes 6291460 | tf_op jit(solution)/shard_map/while
  90.4 13.1 %copy-start.35 = (bf16[64,16,32]{0,2,1:T(8,128)(2,1)S(1)}, bf16[64,16,32]{0,2,1:T(8,128)(2,1)}, u32[]{:S(2)}) copy-start(bf16[64,16,32]{0,2,1:T(8,128)(2,1)} %get-tuple-element.261) | copy-start | bytes 196612 | tf_op jit(solution)/shard_map/while
  131.7 3.1 copy-start.9
  131.7 3.1 copy-start.34
  163.6 11.1 %copy-start.10 = (bf16[2,64,64,32]{2,1,3,0:T(8,128)(2,1)S(1)}, bf16[2,64,64,32]{2,1,3,0:T(8,128)(2,1)}, u32[]{:S(2)}) copy-start(bf16[2,64,64,32]{2,1,3,0:T(8,128)(2,1)} %get-tuple-element.260) | copy-start | bytes 1572868 | tf_op jit(solution)/shard_map/while
  163.6 11.1 %copy-start.25 = (f32[64,16,32]{0,2,1:T(8,128)S(1)}, f32[64,16,32]{0,2,1:T(8,128)}, u32[]{:S(2)}) copy-start(f32[64,16,32]{0,2,1:T(8,128)} %get-tuple-element.247) | copy-start | bytes 393220 | tf_op jit(solution)/shard_map/while
  174.7 13.1 %copy-start.1 = (bf16[64,16,32,32]{3,2,1,0:T(8,128)(2,1)S(1)}, bf16[64,16,32,32]{3,2,1,0:T(8,128)(2,1)}, u32[]{:S(2)}) copy-start(bf16[64,16,32,32]{3,2,1,0:T(8,128)(2,1)} %reshape.157) | copy-start | bytes 6291460 | tf_op jit(solution)/shard_map/while
  174.7 13.1 %copy-start.35 = (bf16[64,16,32]{0,2,1:T(8,128)(2,1)S(1)}, bf16[64,16,32]{0,2,1:T(8,128)(2,1)}, u32[]{:S(2)}) copy-start(bf16[64,16,32]{0,2,1:T(8,128)(2,1)} %get-tuple-element.261) | copy-start | bytes 196612 | tf_op jit(solution)/shard_map/while
  215.8 4.3 %copy-start.2 = (f32[1024,128]{1,0:T(8,128)}, f32[1024,128]{1,0:T(8,128)S(1)}, u32[]{:S(2)}) copy-start(f32[1024,128]{1,0:T(8,128)S(1)} %get-tuple-element.56) | copy-start | bytes 1572868
  215.8 5.1 %copy-start.16 = (f32[64,128]{1,0:T(8,128)S(1)}, f32[64,128]{1,0:T(8,128)}, u32[]{:S(2)}) copy-start(f32[64,128]{1,0:T(8,128)} %copy-done.15) | copy-start | bytes 98308
  215.8 5.2 %copy-start.27 = (f32[64,16,32]{0,2,1:T(8,128)S(1)}, f32[64,16,32]{0,2,1:T(8,128)}, u32[]{:S(2)}) copy-start(f32[64,16,32]{0,2,1:T(8,128)} %get-tuple-element.55) | copy-start | bytes 393220
  215.8 5.5 %copy-start.4 = (bf16[64,16,256]{2,1,0:T(8,128)(2,1)S(1)}, bf16[64,16,256]{2,1,0:T(8,128)(2,1)}, u32[]{:S(2)}) copy-start(bf16[64,16,256]{2,1,0:T(8,128)(2,1)} %param.16) | copy-start | bytes 1572868
  215.8 5.4 %copy-start.12 = (f32[64,16]{1,0:T(8,128)S(1)}, f32[64,16]{1,0:T(8,128)}, u32[]{:S(2)}) copy-start(f32[64,16]{1,0:T(8,128)} %copy-done.11) | copy-start | bytes 12292
  215.8 5.4 %copy-start.22 = (f32[64,16]{1,0:T(8,128)S(1)}, f32[64,16]{1,0:T(8,128)}, u32[]{:S(2)}) copy-start(f32[64,16]{1,0:T(8,128)} %copy-done.21) | copy-start | bytes 12292
  215.8 5.4 %copy-start.33 = (f32[64,16]{1,0:T(8,128)S(1)}, f32[64,16]{1,0:T(8,128)}, u32[]{:S(2)}) copy-start(f32[64,16]{1,0:T(8,128)} %copy-done.32) | copy-start | bytes 12292
  215.8 5.4 %copy-start.40 = (f32[256]{0:T(256)S(1)}, f32[256]{0:T(256)}, u32[]{:S(2)}) copy-start(f32[256]{0:T(256)} %param.21) | copy-start | bytes 3076
  215.8 5.4 %copy-start.42 = (f32[256]{0:T(256)S(1)}, f32[256]{0:T(256)}, u32[]{:S(2)}) copy-start(f32[256]{0:T(256)} %param.22) | copy-start | bytes 3076
  218.7 4.0 %copy-start.24 = (f32[64,16]{1,0:T(8,128)S(1)}, f32[64,16]{1,0:T(8,128)}, u32[]{:S(2)}) copy-start(f32[64,16]{1,0:T(8,128)} %copy-done.23) | copy-start | bytes 12292
  220.0 114.3 %reduce-scatter.8.cloned.1.call-start = ((), (), s32[]{:S(2)}) async-start(), calls=%async_computation.3 | async-start | bytes 557056 | tf_op jit(solution)/shard_map/reduce_scatter | solution.py:176
  220.8 171.7 %reduce-scatter.12.cloned.1.call-start = ((), (), s32[]{:S(2)}) async-start(), calls=%async_computation.5 | async-start | bytes 139264
  221.3 3.5 copy-start.8
  221.3 3.5 copy-start.29
  221.3 3.5 copy-start.37
  251.1 23.3 %copy-start.31 = (bf16[1024,128]{1,0:T(8,128)(2,1)S(1)}, bf16[1024,128]{1,0:T(8,128)(2,1)}, u32[]{:S(2)}) copy-start(bf16[1024,128]{1,0:T(8,128)(2,1)} %param.25) | copy-start | bytes 786436
  251.1 23.3 %copy-start.43 = (f32[128]{0:T(128)S(1)}, f32[128]{0:T(128)}, u32[]{:S(2)}) copy-start(f32[128]{0:T(128)} %param.26) | copy-start | bytes 1540
  274.4 6.3 %copy-start.5 = (bf16[64,8,256]{2,1,0:T(8,128)(2,1)S(1)}, bf16[64,8,256]{2,1,0:T(8,128)(2,1)}, u32[]{:S(2)}) copy-start(bf16[64,8,256]{2,1,0:T(8,128)(2,1)} %param.15) | copy-start | bytes 786436
  274.4 6.3 %copy-start.14 = (f32[64,8]{1,0:T(8,128)S(1)}, f32[64,8]{1,0:T(8,128)}, u32[]{:S(2)}) copy-start(f32[64,8]{1,0:T(8,128)} %copy-done.13) | copy-start | bytes 6148
  274.4 6.3 %copy-start.18 = (f32[64,8]{1,0:T(8,128)S(1)}, f32[64,8]{1,0:T(8,128)}, u32[]{:S(2)}) copy-start(f32[64,8]{1,0:T(8,128)} %copy-done.17) | copy-start | bytes 6148
  274.4 7.4 %copy-start.38 = (bf16[256,32]{0,1:T(8,128)(2,1)S(1)}, bf16[256,32]{0,1:T(8,128)(2,1)}, u32[]{:S(2)}) copy-start(bf16[256,32]{0,1:T(8,128)(2,1)} %param.23) | copy-start | bytes 49156
  274.4 7.7 %copy-start.20 = (f32[64,8]{1,0:T(8,128)S(1)}, f32[64,8]{1,0:T(8,128)}, u32[]{:S(2)}) copy-start(f32[64,8]{1,0:T(8,128)} %copy-done.19) | copy-start | bytes 6148
  (6 other events, 8.2 us)
Sparse Core Ops, SparseCore 0:
  220.2 54.6 reduce-scatter.9
  279.4 54.8 reduce-scatter.7
  338.4 54.0 reduce-scatter.11
where the time goes:
time: 405 us; the launch traced here: 399 us
  local copies, waits for them, and re-layouts  185 us (46%)
  waiting for transfers between devices  110 us (27%)
  matrix products  55.1 us (14%)
  blocking collectives  24.6 us (6%)
  between operations  14.4 us (4%)
  other arithmetic  10.2 us (3%)
    unnamed x5, waiting for transfers between devices  58.9 us
    dynamic_update_slice x4, local copies, waits for them, and re-layouts, per_device(): lax.scan(make_step(), start_index, (left_factor_blocks, denom_blocks, gra...  52.6 us
    reduce_scatter x1, waiting for transfers between devices, per_device(): lax.psum_scatter(weight_sum, 'col', scatter_dimension=0, tiled=True)  50.7 us
    convert_element_type x3, local copies, waits for them, and re-layouts, outer_rows(): outer.astype(jnp.bfloat16).reshape(-1, PROJECTED_WIDTH * PROJECTED_WIDTH)  49.8 us
    reshape x3, local copies, waits for them, and re-layouts, outer_rows(): outer.astype(jnp.bfloat16).reshape(-1, PROJECTED_WIDTH * PROJECTED_WIDTH)  46 us
    dot_general x2, matrix products, step(): jnp.einsum('ijcd,isc->sjd', grad_four, remaining_rows, preferred_element_...  26.1 us
    all_gather x1, blocking collectives, per_device(): current_piece = lax.all_gather(left_outgoing, 'col', axis=0, tiled=True)  24.6 us
    reshape x2, local copies, waits for them, and re-layouts, outer_grad(): grad_outer.reshape(row_inputs, COLUMN_RESIDUES, PROJECTED_WIDTH, PROJECTE...  22.2 us
  transfers between devices with their start and end apart: 3, of which 2 were waited for; matrix products, arithmetic and copies ran while one was open for 16% of the time, Pallas kernels for 0%

commit v1 on v0

--- a/solution.py
+++ b/solution.py
@@ -132,7 +132,12 @@
         jnp.zeros((PROJECTED_WIDTH * PROJECTED_WIDTH, PAIR_WIDTH), jnp.float32),
         jnp.zeros((ALIGNMENT_COUNT, COLUMN_RESIDUES, PROJECTED_WIDTH), jnp.float32),
     )
-    current_piece = lax.all_gather(left_outgoing, "col", axis=0, tiled=True)
+    ring = [left_outgoing]
+    for hop in range(15):
+        ring.append(lax.ppermute(ring[-1], "col", [(dev, (dev + 1) % 16) for dev in range(16)]))
+    current_piece = jnp.roll(
+        jnp.concatenate(ring[::-1], axis=0), (lax.axis_index("col") + 1) * ring[0].shape[0], axis=0
+    )
     row_inputs = current_piece.shape[0]
     remaining_rows = current_piece.reshape(row_inputs, ALIGNMENT_COUNT, PROJECTED_WIDTH)
     rows_denom = denom

time: 405 us -> 447 us (1.10)
  waiting for transfers between devices: 110 us -> 139 us
  loops' own time: 0.46 us -> 13.3 us
  local copies, waits for them, and re-layouts: 185 us -> 180 us
    ppermute x0 -> x15, waiting for transfers between devices: none -> 87.2 us  [per_device(): lax.ppermute(ring[-1], 'col', [(dev, (dev + 1) % 16) for dev in range(16)])]
    reduce_scatter x1, waiting for transfers between devices: 50.7 us -> 0.01 us  [per_device(): lax.psum_scatter(weight_sum, 'col', scatter_dimension=0, tiled=True)]
    another operation x1, loops' own time: 0.46 us -> 13.3 us  [per_device(): lax.scan(make_step(), start_index, (left_factor_blocks, denom_blocks, gra...]
    unnamed x5, waiting for transfers between devices: 58.9 us -> 51.5 us
    reshape x2, local copies, waits for them, and re-layouts: 22.2 us -> 15.9 us  [outer_grad(): grad_outer.reshape(row_inputs, COLUMN_RESIDUES, PROJECTED_WIDTH, PROJECTE...]
    unnamed x80 -> x109, local copies, waits for them, and re-layouts: 8.57 us -> 9.77 us
  transfers between devices with their start and end apart: 3 -> 18, of which waited for: 2 -> 16; matrix products, arithmetic and copies ran while one was open for 16% -> 14% of each run, Pallas kernels for 0% -> 0%
where the time goes in v1:
time: 447 us; the launch traced here: 439 us
  local copies, waits for them, and re-layouts  180 us (40%)
  waiting for transfers between devices  139 us (31%)
  matrix products  56.8 us (13%)
  blocking collectives  24.7 us (6%)
  between operations  15 us (3%)
  loops' own time  13.3 us (3%)
  other arithmetic  10.1 us (2%)
    ppermute x15, waiting for transfers between devices, per_device(): lax.ppermute(ring[-1], 'col', [(dev, (dev + 1) % 16) for dev in range(16)])  87.2 us
    dynamic_update_slice x4, local copies, waits for them, and re-layouts, per_device(): lax.scan(make_step(), start_index, (left_factor_blocks, denom_blocks, gra...  52.6 us
    unnamed x5, waiting for transfers between devices  51.5 us
    convert_element_type x3, local copies, waits for them, and re-layouts, outer_rows(): outer.astype(jnp.bfloat16).reshape(-1, PROJECTED_WIDTH * PROJECTED_WIDTH)  49.9 us
    reshape x3, local copies, waits for them, and re-layouts, outer_rows(): outer.astype(jnp.bfloat16).reshape(-1, PROJECTED_WIDTH * PROJECTED_WIDTH)  45.9 us
    dot_general x2, matrix products, step(): jnp.einsum('ijcd,isc->sjd', grad_four, remaining_rows, preferred_element_...  26.4 us
    all_gather x1, blocking collectives, per_device(): collected_blocks = lax.all_gather(left_outgoing, 'col', axis=0, tiled=True)  24.7 us
    reshape x2, local copies, waits for them, and re-layouts, outer_grad(): grad_outer.reshape(row_inputs, COLUMN_RESIDUES, PROJECTED_WIDTH, PROJECTE...  15.9 us
  transfers between devices with their start and end apart: 18, of which 16 were waited for; matrix products, arithmetic and copies ran while one was open for 14% of the time, Pallas kernels for 0%

profile of v1, /device:TPU:0, one launch (start us, length us, event | category | flops | bytes accessed | tf_op | source)
XLA Modules:
  0.0 439.0 jit_solution(13219011288527759122)
XLA Ops:
  10.3 1.2 fusion.35
  12.7 1.3 fusion.25
  14.3 1.3 convert_reduce_fusion
  15.6 1.4 fusion.26
  17.0 24.7 %all_gather.3 = bf16[128,2048]{1,0:T(8,128)(2,1)S(1)} all-gather(bf16[8,2048]{1,0:T(8,128)(2,1)S(1)} %reshape.128), channel_id=1, replica_groups=mesh['parts'=2,'col'=16] {'col'}, dimensions={0}, use_global_device_ids=true | all-gather | bytes 557056 | tf_op jit(solution)/shard_map/all_gather | solution.py:153
  42.4 2.3 copy.109
  46.3 1.8 copy.108
  48.1 177.1 %while.15 = (s32[]{:T(128)}, f32[1024,128]{1,0:T(8,128)S(1)}, f32[64,16,32]{0,2,1:T(8,128)}, f32[2,64,64,32]{1,0,3,2:T(2,128)}, bf16[2,64,64,32]{2,1,3,0:T(8,128...) while((s32[]{:T(128)}, f32[1024,128]{1,0:T(8,128)S(1)}, ...), condition=%wide.region_5.6_spmd.clone, body=%wide.region_4.5_spmd.clone.sunk | while | flops 944046080 | bytes 45319384 | solution.py:157
  61.1 4.3 fusion.90
  65.5 13.4 %copy.160 = bf16[64,16,32,32]{3,2,1,0:T(8,128)(2,1)} copy(bf16[64,16,32,32]{0,3,1,2:T(8,128)(2,1)} %fusion.90) | data formatting | bytes 4194304 | tf_op jit(solution)/shard_map/while/body/eval_jaxpr/convert_element_type | solution.py:90
  78.9 11.3 %reshape.156 = bf16[1024,1024]{1,0:T(8,128)(2,1)S(1)} reshape(bf16[64,16,32,32]{3,2,1,0:T(8,128)(2,1)} %copy.160) | data formatting | bytes 4194304 | tf_op jit(solution)/shard_map/while/body/eval_jaxpr/reshape | solution.py:90
  91.3 1.7 divide_convert_fusion.3
  92.9 8.0 %reshape.157 = bf16[64,16,32,32]{3,2,1,0:T(8,128)(2,1)} reshape(bf16[1024,1024]{1,0:T(8,128)(2,1)S(1)} %divide_convert_fusion.3) | data formatting | bytes 4194304 | tf_op jit(solution)/shard_map/while/body/eval_jaxpr/reshape | solution.py:100
  100.9 13.2 %fusion.91 = f32[64,16,32]{0,2,1:T(8,128)S(1)} fusion(bf16[64,16,32,32]{3,2,1,0:T(8,128)(2,1)} %reshape.157, bf16[2,64,64,32]{2,1,3,0:T(8,128)(2,1)} %get-tuple-element.260, s32[]{:T(128)} %get-tuple-element.245, f32[64,16,32]{0,2,1:T(8,128)S(1)} %copy-done.23, pred[]{:T(512)S(6)} %compare.4), kind=kOutput, calls=%fused_computation.8.clone.1 | convolution fusion | flops 134283264 | bytes 9175553 | tf_op jit(solution)/shard_map/while/body/eval_jaxpr/ijcd,isc->sjd/dot_general | solution.py:113
  114.1 2.7 convolution_bitcast_fusion.5
  117.7 25.5 %dynamic_update_slice.6 = f32[2,64,64,32]{1,0,3,2:T(2,128)} dynamic-update-slice(f32[2,64,64,32]{1,0,3,2:T(2,128)} %get-tuple-element.248, f32[1,64,64,32]{1,0,3,2:T(1,128)S(1)} %copy.162, s32[]{:T(128)} %get-tuple-element.245, s32[]{:T(128)} %constant.60.clone.1..sunk, s32[]{:T(128)} %constant.60.clone.1..sunk, s32[]{:T(128)} %constant.60.clone.1..sunk) | dynamic-update-slice | bytes 1048580 | tf_op jit(solution)/shard_map/while/body/jit(dynamic_update_index_in_dim)/dynamic_update_slice | solution.py:157
  143.2 4.3 fusion.90
  147.5 13.4 %copy.160 = bf16[64,16,32,32]{3,2,1,0:T(8,128)(2,1)} copy(bf16[64,16,32,32]{0,3,1,2:T(8,128)(2,1)} %fusion.90) | data formatting | bytes 4194304 | tf_op jit(solution)/shard_map/while/body/eval_jaxpr/convert_element_type | solution.py:90
  160.9 11.3 %reshape.156 = bf16[1024,1024]{1,0:T(8,128)(2,1)S(1)} reshape(bf16[64,16,32,32]{3,2,1,0:T(8,128)(2,1)} %copy.160) | data formatting | bytes 4194304 | tf_op jit(solution)/shard_map/while/body/eval_jaxpr/reshape | solution.py:90
  173.3 1.7 divide_convert_fusion.3
  174.9 8.0 %reshape.157 = bf16[64,16,32,32]{3,2,1,0:T(8,128)(2,1)} reshape(bf16[1024,1024]{1,0:T(8,128)(2,1)S(1)} %divide_convert_fusion.3) | data formatting | bytes 4194304 | tf_op jit(solution)/shard_map/while/body/eval_jaxpr/reshape | solution.py:100
  182.9 13.2 %fusion.91 = f32[64,16,32]{0,2,1:T(8,128)S(1)} fusion(bf16[64,16,32,32]{3,2,1,0:T(8,128)(2,1)} %reshape.157, bf16[2,64,64,32]{2,1,3,0:T(8,128)(2,1)} %get-tuple-element.260, s32[]{:T(128)} %get-tuple-element.245, f32[64,16,32]{0,2,1:T(8,128)S(1)} %copy-done.23, pred[]{:T(512)S(6)} %compare.4), kind=kOutput, calls=%fused_computation.8.clone.1 | convolution fusion | flops 134283264 | bytes 9175553 | tf_op jit(solution)/shard_map/while/body/eval_jaxpr/ijcd,isc->sjd/dot_general | solution.py:113
  196.1 2.7 convolution_bitcast_fusion.5
  199.7 25.5 %dynamic_update_slice.6 = f32[2,64,64,32]{1,0,3,2:T(2,128)} dynamic-update-slice(f32[2,64,64,32]{1,0,3,2:T(2,128)} %get-tuple-element.248, f32[1,64,64,32]{1,0,3,2:T(1,128)S(1)} %copy.162, s32[]{:T(128)} %get-tuple-element.245, s32[]{:T(128)} %constant.60.clone.1..sunk, s32[]{:T(128)} %constant.60.clone.1..sunk, s32[]{:T(128)} %constant.60.clone.1..sunk) | dynamic-update-slice | bytes 1048580 | tf_op jit(solution)/shard_map/while/body/jit(dynamic_update_index_in_dim)/dynamic_update_slice | solution.py:157
  225.2 2.8 reshape.135
  228.1 1.4 copy.128
  229.9 5.7 %collective-permute-done = bf16[8,2048]{1,0:T(8,128)(2,1)S(1)} collective-permute-done((bf16[8,2048]{1,0:T(8,128)(2,1)S(1)}, bf16[8,2048]{1,0:T(8,128)(2,1)S(1)}, u32[]{:S(2)}, u32[]{:S(2)}) %collective-permute-start) | collective-permute-done | bytes 32800 | tf_op jit(solution)/shard_map/ppermute | solution.py:137
  235.6 6.0 %collective-permute-done.1 = bf16[8,2048]{1,0:T(8,128)(2,1)S(1)} collective-permute-done((bf16[8,2048]{1,0:T(8,128)(2,1)S(1)}, bf16[8,2048]{1,0:T(8,128)(2,1)S(1)}, u32[]{:S(2)}, u32[]{:S(2)}) %collective-permute-start.1) | collective-permute-done | bytes 32800 | tf_op jit(solution)/shard_map/ppermute | solution.py:137
  241.6 6.0 %collective-permute-done.2 = bf16[8,2048]{1,0:T(8,128)(2,1)S(1)} collective-permute-done((bf16[8,2048]{1,0:T(8,128)(2,1)S(1)}, bf16[8,2048]{1,0:T(8,128)(2,1)S(1)}, u32[]{:S(2)}, u32[]{:S(2)}) %collective-permute-start.2) | collective-permute-done | bytes 32800 | tf_op jit(solution)/shard_map/ppermute | solution.py:137
  247.7 6.0 %collective-permute-done.3 = bf16[8,2048]{1,0:T(8,128)(2,1)S(1)} collective-permute-done((bf16[8,2048]{1,0:T(8,128)(2,1)S(1)}, bf16[8,2048]{1,0:T(8,128)(2,1)S(1)}, u32[]{:S(2)}, u32[]{:S(2)}) %collective-permute-start.3) | collective-permute-done | bytes 32800 | tf_op jit(solution)/shard_map/ppermute | solution.py:137
  253.7 6.4 %collective-permute-done.4 = bf16[8,2048]{1,0:T(8,128)(2,1)S(1)} collective-permute-done((bf16[8,2048]{1,0:T(8,128)(2,1)S(1)}, bf16[8,2048]{1,0:T(8,128)(2,1)S(1)}, u32[]{:S(2)}, u32[]{:S(2)}) %collective-permute-start.4) | collective-permute-done | bytes 32800 | tf_op jit(solution)/shard_map/ppermute | solution.py:137
  260.1 6.1 %collective-permute-done.5 = bf16[8,2048]{1,0:T(8,128)(2,1)S(1)} collective-permute-done((bf16[8,2048]{1,0:T(8,128)(2,1)S(1)}, bf16[8,2048]{1,0:T(8,128)(2,1)S(1)}, u32[]{:S(2)}, u32[]{:S(2)}) %collective-permute-start.5) | collective-permute-done | bytes 32800 | tf_op jit(solution)/shard_map/ppermute | solution.py:137
  266.3 6.0 %collective-permute-done.6 = bf16[8,2048]{1,0:T(8,128)(2,1)S(1)} collective-permute-done((bf16[8,2048]{1,0:T(8,128)(2,1)S(1)}, bf16[8,2048]{1,0:T(8,128)(2,1)S(1)}, u32[]{:S(2)}, u32[]{:S(2)}) %collective-permute-start.6) | collective-permute-done | bytes 32800 | tf_op jit(solution)/shard_map/ppermute | solution.py:137
  272.7 5.6 %collective-permute-done.7 = bf16[8,2048]{1,0:T(8,128)(2,1)S(1)} collective-permute-done((bf16[8,2048]{1,0:T(8,128)(2,1)S(1)}, bf16[8,2048]{1,0:T(8,128)(2,1)S(1)}, u32[]{:S(2)}, u32[]{:S(2)}) %collective-permute-start.7) | collective-permute-done | bytes 32800 | tf_op jit(solution)/shard_map/ppermute | solution.py:137
  278.9 5.6 %collective-permute-done.8 = bf16[8,2048]{1,0:T(8,128)(2,1)S(1)} collective-permute-done((bf16[8,2048]{1,0:T(8,128)(2,1)S(1)}, bf16[8,2048]{1,0:T(8,128)(2,1)S(1)}, u32[]{:S(2)}, u32[]{:S(2)}) %collective-permute-start.8) | collective-permute-done | bytes 32800 | tf_op jit(solution)/shard_map/ppermute | solution.py:137
  284.5 6.0 %collective-permute-done.9 = bf16[8,2048]{1,0:T(8,128)(2,1)S(1)} collective-permute-done((bf16[8,2048]{1,0:T(8,128)(2,1)S(1)}, bf16[8,2048]{1,0:T(8,128)(2,1)S(1)}, u32[]{:S(2)}, u32[]{:S(2)}) %collective-permute-start.9) | collective-permute-done | bytes 32800 | tf_op jit(solution)/shard_map/ppermute | solution.py:137
  291.2 5.4 %collective-permute-done.10 = bf16[8,2048]{1,0:T(8,128)(2,1)S(1)} collective-permute-done((bf16[8,2048]{1,0:T(8,128)(2,1)S(1)}, bf16[8,2048]{1,0:T(8,128)(2,1)S(1)}, u32[]{:S(2)}, u32[]{:S(2)}) %collective-permute-start.10) | collective-permute-done | bytes 32800 | tf_op jit(solution)/shard_map/ppermute | solution.py:137
  296.6 6.0 %collective-permute-done.11 = bf16[8,2048]{1,0:T(8,128)(2,1)S(1)} collective-permute-done((bf16[8,2048]{1,0:T(8,128)(2,1)S(1)}, bf16[8,2048]{1,0:T(8,128)(2,1)S(1)}, u32[]{:S(2)}, u32[]{:S(2)}) %collective-permute-start.11) | collective-permute-done | bytes 32800 | tf_op jit(solution)/shard_map/ppermute | solution.py:137
  302.6 1.4 add_convert_fusion
  304.0 4.6 %collective-permute-done.12 = bf16[8,2048]{1,0:T(8,128)(2,1)S(1)} collective-permute-done((bf16[8,2048]{1,0:T(8,128)(2,1)S(1)}, bf16[8,2048]{1,0:T(8,128)(2,1)S(1)}, u32[]{:S(2)}, u32[]{:S(2)}) %collective-permute-start.12) | collective-permute-done | bytes 32800 | tf_op jit(solution)/shard_map/ppermute | solution.py:137
  309.4 5.3 %collective-permute-done.13 = bf16[8,2048]{1,0:T(8,128)(2,1)S(1)} collective-permute-done((bf16[8,2048]{1,0:T(8,128)(2,1)S(1)}, bf16[8,2048]{1,0:T(8,128)(2,1)S(1)}, u32[]{:S(2)}, u32[]{:S(2)}) %collective-permute-start.13) | collective-permute-done | bytes 32800 | tf_op jit(solution)/shard_map/ppermute | solution.py:137
  314.8 6.3 %collective-permute-done.14 = bf16[8,2048]{1,0:T(8,128)(2,1)S(1)} collective-permute-done((bf16[8,2048]{1,0:T(8,128)(2,1)S(1)}, bf16[8,2048]{1,0:T(8,128)(2,1)S(1)}, u32[]{:S(2)}, u32[]{:S(2)}) %collective-permute-start.14) | collective-permute-done | bytes 32800 | tf_op jit(solution)/shard_map/ppermute | solution.py:137
  321.8 3.2 fusion.17
  325.1 23.1 %copy.106 = bf16[128,16,32,32]{3,2,1,0:T(8,128)(2,1)} copy(bf16[128,16,32,32]{0,3,2,1:T(8,128)(2,1)} %fusion.17) | data formatting | bytes 8388608 | tf_op jit(solution)/shard_map/convert_element_type | solution.py:90
  348.2 23.3 %reshape.130 = bf16[2048,1024]{1,0:T(8,128)(2,1)} reshape(bf16[128,16,32,32]{3,2,1,0:T(8,128)(2,1)} %copy.106) | data formatting | bytes 8388608 | tf_op jit(solution)/shard_map/reshape | solution.py:90
  371.5 4.3 fusion.18
  375.8 1.2 copy.129
  380.7 51.4 %reduce-scatter.12.cloned.1.call-done = f32[16,64]{1,0:T(8,128)} async-done(((f32[256,64]{1,0:T(8,128)}), f32[16,64]{1,0:T(8,128)}) %reduce-scatter.12.cloned.1.call-update) | async-done | bytes 4112
  (192 shorter events, 17.5 us)
Async XLA Ops:
  7.2 37.6 %copy-start = (bf16[256,32]{0,1:T(8,128)(2,1)S(1)}, bf16[256,32]{0,1:T(8,128)(2,1)}, u32[]{:S(2)}) copy-start(bf16[256,32]{0,1:T(8,128)(2,1)} %param.24) | copy-start | bytes 49156
  7.2 368.6 %reduce-scatter.10.cloned.1.call-start = ((), (), s32[]{:S(2)}) async-start(), calls=%async_computation.4 | async-start | bytes 1114112
  8.1 36.6 %copy-start.29 = (f32[64,16]{1,0:T(8,128)}, f32[64,16]{1,0:T(8,128)S(1)}, u32[]{:S(2)}) copy-start(f32[64,16]{1,0:T(8,128)S(1)} %copy.101) | copy-start | bytes 12292
  9.1 37.1 %copy-start.31 = (f32[128,16]{0,1:T(8,128)}, f32[128,16]{0,1:T(8,128)S(1)}, u32[]{:S(2)}) copy-start(f32[128,16]{0,1:T(8,128)S(1)} %convolution_maximum_fusion) | copy-start | bytes 24580
  12.7 32.0 %copy-start.3 = (bf16[64,16,256]{2,1,0:T(8,128)(2,1)S(1)}, bf16[64,16,256]{2,1,0:T(8,128)(2,1)}, u32[]{:S(2)}) copy-start(bf16[64,16,256]{2,1,0:T(8,128)(2,1)} %param.16) | copy-start | bytes 1572868
  12.7 32.0 %copy-start.34 = (f32[256]{0:T(256)S(1)}, f32[256]{0:T(256)}, u32[]{:S(2)}) copy-start(f32[256]{0:T(256)} %param.21) | copy-start | bytes 3076
  12.7 32.1 %copy-start.36 = (f32[256]{0:T(256)S(1)}, f32[256]{0:T(256)}, u32[]{:S(2)}) copy-start(f32[256]{0:T(256)} %param.22) | copy-start | bytes 3076
  14.3 31.0 %copy-start.11 = (bf16[8,2048]{1,0:T(8,128)(2,1)}, bf16[8,2048]{1,0:T(8,128)(2,1)S(1)}, u32[]{:S(2)}) copy-start(bf16[8,2048]{1,0:T(8,128)(2,1)S(1)} %reshape.128) | copy-start | bytes 98308
  15.5 30.7 %copy-start.7 = (f32[64,16]{1,0:T(8,128)}, f32[64,16]{1,0:T(8,128)S(1)}, u32[]{:S(2)}) copy-start(f32[64,16]{1,0:T(8,128)S(1)} %broadcast_multiply_fusion.1) | copy-start | bytes 12292
  17.0 31.1 %copy-start.21 = (f32[64,16]{1,0:T(8,128)}, f32[64,16]{1,0:T(8,128)S(1)}, u32[]{:S(2)}) copy-start(f32[64,16]{1,0:T(8,128)S(1)} %fusion.26) | copy-start | bytes 12292
  17.0 31.1 %copy-start.6 = (bf16[128,16,128]{2,1,0:T(8,128)(2,1)S(1)}, bf16[128,16,128]{2,1,0:T(8,128)(2,1)}, u32[]{:S(2)}) copy-start(bf16[128,16,128]{2,1,0:T(8,128)(2,1)} %param.27) | copy-start | bytes 1572868
  17.0 31.0 %copy-start.19 = (f32[64,16]{1,0:T(8,128)}, f32[64,16]{1,0:T(8,128)S(1)}, u32[]{:S(2)}) copy-start(f32[64,16]{1,0:T(8,128)S(1)} %fusion.50) | copy-start | bytes 12292
  92.9 8.0 %copy-start.23 = (f32[64,16,32]{0,2,1:T(8,128)S(1)}, f32[64,16,32]{0,2,1:T(8,128)}, u32[]{:S(2)}) copy-start(f32[64,16,32]{0,2,1:T(8,128)} %get-tuple-element.247) | copy-start | bytes 393220 | tf_op jit(solution)/shard_map/while
  100.9 13.2 %copy-start.1 = (bf16[64,16,32,32]{3,2,1,0:T(8,128)(2,1)S(1)}, bf16[64,16,32,32]{3,2,1,0:T(8,128)(2,1)}, u32[]{:S(2)}) copy-start(bf16[64,16,32,32]{3,2,1,0:T(8,128)(2,1)} %reshape.157) | copy-start | bytes 6291460 | tf_op jit(solution)/shard_map/while
  174.9 8.0 %copy-start.23 = (f32[64,16,32]{0,2,1:T(8,128)S(1)}, f32[64,16,32]{0,2,1:T(8,128)}, u32[]{:S(2)}) copy-start(f32[64,16,32]{0,2,1:T(8,128)} %get-tuple-element.247) | copy-start | bytes 393220 | tf_op jit(solution)/shard_map/while
  182.9 13.2 %copy-start.1 = (bf16[64,16,32,32]{3,2,1,0:T(8,128)(2,1)S(1)}, bf16[64,16,32,32]{3,2,1,0:T(8,128)(2,1)}, u32[]{:S(2)}) copy-start(bf16[64,16,32,32]{3,2,1,0:T(8,128)(2,1)} %reshape.157) | copy-start | bytes 6291460 | tf_op jit(solution)/shard_map/while
  225.1 47.2 %copy-start.2 = (f32[1024,128]{1,0:T(8,128)}, f32[1024,128]{1,0:T(8,128)S(1)}, u32[]{:S(2)}) copy-start(f32[1024,128]{1,0:T(8,128)S(1)} %get-tuple-element.56) | copy-start | bytes 1572868
  225.1 47.3 %copy-start.25 = (f32[64,16,32]{0,2,1:T(8,128)S(1)}, f32[64,16,32]{0,2,1:T(8,128)}, u32[]{:S(2)}) copy-start(f32[64,16,32]{0,2,1:T(8,128)} %get-tuple-element.55) | copy-start | bytes 393220
  225.2 53.2 %copy-start.4 = (bf16[64,16,256]{2,1,0:T(8,128)(2,1)S(1)}, bf16[64,16,256]{2,1,0:T(8,128)(2,1)}, u32[]{:S(2)}) copy-start(bf16[64,16,256]{2,1,0:T(8,128)(2,1)} %param.16) | copy-start | bytes 1572868
  225.2 53.2 %copy-start.8 = (f32[64,16]{1,0:T(8,128)S(1)}, f32[64,16]{1,0:T(8,128)}, u32[]{:S(2)}) copy-start(f32[64,16]{1,0:T(8,128)} %copy-done.7) | copy-start | bytes 12292
  225.2 53.2 %copy-start.30 = (f32[64,16]{1,0:T(8,128)S(1)}, f32[64,16]{1,0:T(8,128)}, u32[]{:S(2)}) copy-start(f32[64,16]{1,0:T(8,128)} %copy-done.29) | copy-start | bytes 12292
  225.2 53.2 %copy-start.35 = (f32[256]{0:T(256)S(1)}, f32[256]{0:T(256)}, u32[]{:S(2)}) copy-start(f32[256]{0:T(256)} %param.21) | copy-start | bytes 3076
  225.2 59.3 %copy-start.22 = (f32[64,16]{1,0:T(8,128)S(1)}, f32[64,16]{1,0:T(8,128)}, u32[]{:S(2)}) copy-start(f32[64,16]{1,0:T(8,128)} %copy-done.21) | copy-start | bytes 12292
  225.2 65.3 %copy-start.20 = (f32[64,16]{1,0:T(8,128)S(1)}, f32[64,16]{1,0:T(8,128)}, u32[]{:S(2)}) copy-start(f32[64,16]{1,0:T(8,128)} %copy-done.19) | copy-start | bytes 12292
  229.4 79.2 %copy-start.37 = (f32[256]{0:T(256)S(1)}, f32[256]{0:T(256)}, u32[]{:S(2)}) copy-start(f32[256]{0:T(256)} %param.22) | copy-start | bytes 3076
  229.4 151.3 %reduce-scatter.8.cloned.1.call-start = ((), (), s32[]{:S(2)}) async-start(), calls=%async_computation.3 | async-start | bytes 557056 | tf_op jit(solution)/shard_map/reduce_scatter | solution.py:181
  229.5 6.1 %collective-permute-start = (bf16[8,2048]{1,0:T(8,128)(2,1)S(1)}, bf16[8,2048]{1,0:T(8,128)(2,1)S(1)}, u32[]{:S(2)}, u32[]{:S(2)}) collective-permute-start(bf16[8,2048]{1,0:T(8,128)(2,1)S(1)} %copy-done.12), channel_id=1, source_target_pairs={{0,1},{1,2},{2,3},{3,4},{4,5},{5,6},{6,7},{7,8},{8,9},{9,10},{10,1... | collective-permute-start | bytes 98312 | tf_op jit(solution)/shard_map/ppermute | solution.py:137
  235.6 6.0 %collective-permute-start.1 = (bf16[8,2048]{1,0:T(8,128)(2,1)S(1)}, bf16[8,2048]{1,0:T(8,128)(2,1)S(1)}, u32[]{:S(2)}, u32[]{:S(2)}) collective-permute-start(bf16[8,2048]{1,0:T(8,128)(2,1)S(1)} %collective-permute-done), channel_id=1, source_target_pairs={{0,1},{1,2},{2,3},{3,4},{4,5},{5,6},{6,7},{7,8},{8,9},{9,10},{10,1... | collective-permute-start | bytes 98312 | tf_op jit(solution)/shard_map/ppermute | solution.py:137
  241.6 6.0 %collective-permute-start.2 = (bf16[8,2048]{1,0:T(8,128)(2,1)S(1)}, bf16[8,2048]{1,0:T(8,128)(2,1)S(1)}, u32[]{:S(2)}, u32[]{:S(2)}) collective-permute-start(bf16[8,2048]{1,0:T(8,128)(2,1)S(1)} %collective-permute-done.1), channel_id=1, source_target_pairs={{0,1},{1,2},{2,3},{3,4},{4,5},{5,6},{6,7},{7,8},{8,9},{9,10},{10,1... | collective-permute-start | bytes 98312 | tf_op jit(solution)/shard_map/ppermute | solution.py:137
  247.7 6.0 %collective-permute-start.3 = (bf16[8,2048]{1,0:T(8,128)(2,1)S(1)}, bf16[8,2048]{1,0:T(8,128)(2,1)S(1)}, u32[]{:S(2)}, u32[]{:S(2)}) collective-permute-start(bf16[8,2048]{1,0:T(8,128)(2,1)S(1)} %collective-permute-done.2), channel_id=1, source_target_pairs={{0,1},{1,2},{2,3},{3,4},{4,5},{5,6},{6,7},{7,8},{8,9},{9,10},{10,1... | collective-permute-start | bytes 98312 | tf_op jit(solution)/shard_map/ppermute | solution.py:137
  253.7 6.4 %collective-permute-start.4 = (bf16[8,2048]{1,0:T(8,128)(2,1)S(1)}, bf16[8,2048]{1,0:T(8,128)(2,1)S(1)}, u32[]{:S(2)}, u32[]{:S(2)}) collective-permute-start(bf16[8,2048]{1,0:T(8,128)(2,1)S(1)} %collective-permute-done.3), channel_id=1, source_target_pairs={{0,1},{1,2},{2,3},{3,4},{4,5},{5,6},{6,7},{7,8},{8,9},{9,10},{10,1... | collective-permute-start | bytes 98312 | tf_op jit(solution)/shard_map/ppermute | solution.py:137
  260.1 6.2 %collective-permute-start.5 = (bf16[8,2048]{1,0:T(8,128)(2,1)S(1)}, bf16[8,2048]{1,0:T(8,128)(2,1)S(1)}, u32[]{:S(2)}, u32[]{:S(2)}) collective-permute-start(bf16[8,2048]{1,0:T(8,128)(2,1)S(1)} %collective-permute-done.4), channel_id=1, source_target_pairs={{0,1},{1,2},{2,3},{3,4},{4,5},{5,6},{6,7},{7,8},{8,9},{9,10},{10,1... | collective-permute-start | bytes 98312 | tf_op jit(solution)/shard_map/ppermute | solution.py:137
  266.3 6.0 %collective-permute-start.6 = (bf16[8,2048]{1,0:T(8,128)(2,1)S(1)}, bf16[8,2048]{1,0:T(8,128)(2,1)S(1)}, u32[]{:S(2)}, u32[]{:S(2)}) collective-permute-start(bf16[8,2048]{1,0:T(8,128)(2,1)S(1)} %collective-permute-done.5), channel_id=1, source_target_pairs={{0,1},{1,2},{2,3},{3,4},{4,5},{5,6},{6,7},{7,8},{8,9},{9,10},{10,1... | collective-permute-start | bytes 98312 | tf_op jit(solution)/shard_map/ppermute | solution.py:137
  272.3 6.0 %collective-permute-start.7 = (bf16[8,2048]{1,0:T(8,128)(2,1)S(1)}, bf16[8,2048]{1,0:T(8,128)(2,1)S(1)}, u32[]{:S(2)}, u32[]{:S(2)}) collective-permute-start(bf16[8,2048]{1,0:T(8,128)(2,1)S(1)} %collective-permute-done.6), channel_id=1, source_target_pairs={{0,1},{1,2},{2,3},{3,4},{4,5},{5,6},{6,7},{7,8},{8,9},{9,10},{10,1... | collective-permute-start | bytes 98312 | tf_op jit(solution)/shard_map/ppermute | solution.py:137
  272.4 159.7 %reduce-scatter.12.cloned.1.call-start = ((), (), s32[]{:S(2)}) async-start(), calls=%async_computation.5 | async-start | bytes 139264
  272.7 42.0 %copy-start.14 = (f32[64,128]{1,0:T(8,128)S(1)}, f32[64,128]{1,0:T(8,128)}, u32[]{:S(2)}) copy-start(f32[64,128]{1,0:T(8,128)} %copy-done.13) | copy-start | bytes 98308
  278.4 6.1 %collective-permute-start.8 = (bf16[8,2048]{1,0:T(8,128)(2,1)S(1)}, bf16[8,2048]{1,0:T(8,128)(2,1)S(1)}, u32[]{:S(2)}, u32[]{:S(2)}) collective-permute-start(bf16[8,2048]{1,0:T(8,128)(2,1)S(1)} %collective-permute-done.7), channel_id=1, source_target_pairs={{0,1},{1,2},{2,3},{3,4},{4,5},{5,6},{6,7},{7,8},{8,9},{9,10},{10,1... | collective-permute-start | bytes 98312 | tf_op jit(solution)/shard_map/ppermute | solution.py:137
  284.5 6.0 %collective-permute-start.9 = (bf16[8,2048]{1,0:T(8,128)(2,1)S(1)}, bf16[8,2048]{1,0:T(8,128)(2,1)S(1)}, u32[]{:S(2)}, u32[]{:S(2)}) collective-permute-start(bf16[8,2048]{1,0:T(8,128)(2,1)S(1)} %collective-permute-done.8), channel_id=1, source_target_pairs={{0,1},{1,2},{2,3},{3,4},{4,5},{5,6},{6,7},{7,8},{8,9},{9,10},{10,1... | collective-permute-start | bytes 98312 | tf_op jit(solution)/shard_map/ppermute | solution.py:137
  290.5 6.0 %collective-permute-start.10 = (bf16[8,2048]{1,0:T(8,128)(2,1)S(1)}, bf16[8,2048]{1,0:T(8,128)(2,1)S(1)}, u32[]{:S(2)}, u32[]{:S(2)}) collective-permute-start(bf16[8,2048]{1,0:T(8,128)(2,1)S(1)} %collective-permute-done.9), channel_id=1, source_target_pairs={{0,1},{1,2},{2,3},{3,4},{4,5},{5,6},{6,7},{7,8},{8,9},{9,10},{10,1... | collective-permute-start | bytes 98312 | tf_op jit(solution)/shard_map/ppermute | solution.py:137
  296.6 6.0 %collective-permute-start.11 = (bf16[8,2048]{1,0:T(8,128)(2,1)S(1)}, bf16[8,2048]{1,0:T(8,128)(2,1)S(1)}, u32[]{:S(2)}, u32[]{:S(2)}) collective-permute-start(bf16[8,2048]{1,0:T(8,128)(2,1)S(1)} %collective-permute-done.10), channel_id=1, source_target_pairs={{0,1},{1,2},{2,3},{3,4},{4,5},{5,6},{6,7},{7,8},{8,9},{9,10},{10,1... | collective-permute-start | bytes 98312 | tf_op jit(solution)/shard_map/ppermute | solution.py:137
  296.6 25.2 %copy-start.27 = (bf16[64,16,32]{2,1,0:T(8,128)(2,1)S(1)}, bf16[64,16,32]{2,1,0:T(8,128)(2,1)}, u32[]{:S(2)}) copy-start(bf16[64,16,32]{2,1,0:T(8,128)(2,1)} %copy-done.26) | copy-start | bytes 196612
  296.6 25.2 %copy-start.32 = (f32[128,16]{0,1:T(8,128)S(1)}, f32[128,16]{0,1:T(8,128)}, u32[]{:S(2)}) copy-start(f32[128,16]{0,1:T(8,128)} %copy-done.31) | copy-start | bytes 24580
  302.6 6.0 %collective-permute-start.12 = (bf16[8,2048]{1,0:T(8,128)(2,1)S(1)}, bf16[8,2048]{1,0:T(8,128)(2,1)S(1)}, u32[]{:S(2)}, u32[]{:S(2)}) collective-permute-start(bf16[8,2048]{1,0:T(8,128)(2,1)S(1)} %collective-permute-done.11), channel_id=1, source_target_pairs={{0,1},{1,2},{2,3},{3,4},{4,5},{5,6},{6,7},{7,8},{8,9},{9,10},{10,1... | collective-permute-start | bytes 98312 | tf_op jit(solution)/shard_map/ppermute | solution.py:137
  308.6 6.0 %collective-permute-start.13 = (bf16[8,2048]{1,0:T(8,128)(2,1)S(1)}, bf16[8,2048]{1,0:T(8,128)(2,1)S(1)}, u32[]{:S(2)}, u32[]{:S(2)}) collective-permute-start(bf16[8,2048]{1,0:T(8,128)(2,1)S(1)} %collective-permute-done.12), channel_id=1, source_target_pairs={{0,1},{1,2},{2,3},{3,4},{4,5},{5,6},{6,7},{7,8},{8,9},{9,10},{10,1... | collective-permute-start | bytes 98312 | tf_op jit(solution)/shard_map/ppermute | solution.py:137
  314.7 6.4 %collective-permute-start.14 = (bf16[8,2048]{1,0:T(8,128)(2,1)S(1)}, bf16[8,2048]{1,0:T(8,128)(2,1)S(1)}, u32[]{:S(2)}, u32[]{:S(2)}) collective-permute-start(bf16[8,2048]{1,0:T(8,128)(2,1)S(1)} %collective-permute-done.13), channel_id=1, source_target_pairs={{0,1},{1,2},{2,3},{3,4},{4,5},{5,6},{6,7},{7,8},{8,9},{9,10},{10,1... | collective-permute-start | bytes 98312 | tf_op jit(solution)/shard_map/ppermute | solution.py:137
  348.2 23.3 %copy-start.28 = (bf16[1024,128]{1,0:T(8,128)(2,1)S(1)}, bf16[1024,128]{1,0:T(8,128)(2,1)}, u32[]{:S(2)}) copy-start(bf16[1024,128]{1,0:T(8,128)(2,1)} %param.25) | copy-start | bytes 786436
  348.2 23.3 %copy-start.38 = (f32[128]{0:T(128)S(1)}, f32[128]{0:T(128)}, u32[]{:S(2)}) copy-start(f32[128]{0:T(128)} %param.26) | copy-start | bytes 1540
  371.5 7.7 %copy-start.18 = (f32[64,8]{1,0:T(8,128)S(1)}, f32[64,8]{1,0:T(8,128)}, u32[]{:S(2)}) copy-start(f32[64,8]{1,0:T(8,128)} %copy-done.17) | copy-start | bytes 6148
  (12 other events, 49.3 us)
Sparse Core Ops, SparseCore 0:
  229.6 55.0 reduce-scatter.9
  289.2 54.8 reduce-scatter.7
  379.8 52.2 reduce-scatter.11
